TPU v7x, 256 devices: a whole 4x4x8 slice. The times are simulated.
256 devices in a mesh: fsdp: 64 (over x, z, core), rep: 4 (over y).
Axes of the slice: x: 4, y: 4, z: 8, core: 2. Of those that a mesh axis runs over, the one named last changes fastest.
Arguments:
- grad: bfloat16 [128, 256, 2048], P(None, 'fsdp'), may hold values from -6 to 6
- momentum: float32 [128, 256, 2048], P(None, 'fsdp'), may hold values from -6 to 6
- owner_list: int32 [128], replicated, may hold values from 0 to 63, as said below
Outputs:
- new_momentum: float32 [128, 256, 2048], P(None, 'fsdp')
- update: bfloat16 [128, 256, 2048], P(None, 'fsdp')
- owned_update: bfloat16 [256, 256, 2048], P(('fsdp', 'rep'))
Inputs may be any that keep to these rules, and one draw needn't show every extreme that they name: `owner_list`: no owner is named by more than 4 matrices; some owner is named by exactly 4 in every draw.
All inputs are finite; a program needn't handle non-finite values.
Results may differ from a plain program's by a relative error of at most 0.03.
Values may be sent and summed in bfloat16 or wider, within the bound.
A program may use at most 128 MiB of HBM per device.

v0:
```python
import jax
import jax.numpy as jnp
from jax import lax
from jax.sharding import PartitionSpec as P

CAP = 4
ITERS = 5
decay_rate = 0.95
norm_eps = 1e-07
quintic_a = 3.4445
quintic_b = -4.775
quintic_c = 2.0315


def newton(blended):
    values = blended.astype(jnp.float32)
    total = jnp.sqrt(jnp.sum(values * values))
    current = (values / (total + norm_eps)).astype(jnp.bfloat16)
    for iteration in range(ITERS):
        gram = jnp.dot(current, current.T, preferred_element_type=jnp.float32).astype(jnp.bfloat16)
        square = jnp.dot(gram, gram, preferred_element_type=jnp.float32)
        poly = (quintic_b * gram.astype(jnp.float32) + quintic_c * square).astype(jnp.bfloat16)
        applied = jnp.dot(poly, current, preferred_element_type=jnp.float32)
        current = (quintic_a * current.astype(jnp.float32) + applied).astype(jnp.bfloat16)
    return current


def local(grad, momentum, owner_list):
    matrix_count, row_count, col_count = grad.shape
    owner_count = lax.axis_size("fsdp")
    replicas = lax.axis_size("rep")
    capacity = CAP
    per_replica = capacity // replicas
    replica = lax.axis_index("rep")
    new_momentum = decay_rate * momentum + grad.astype(jnp.float32)
    blended = (grad.astype(jnp.float32) + decay_rate * new_momentum).astype(jnp.bfloat16)
    order = jnp.arange(matrix_count)
    earlier = order[None, :] < order[:, None]
    same_owner = owner_list[None, :] == owner_list[:, None]
    slot_index = jnp.sum(jnp.logical_and(earlier, same_owner), axis=1)
    position = slot_index * owner_count + owner_list
    targets = jnp.arange(capacity * owner_count)
    matched = position[None, :] == targets[:, None]
    sources = jnp.sum(jnp.where(matched, order[None, :], 0), axis=1)
    filled = jnp.any(matched, axis=1)
    flattened = blended.reshape(matrix_count, row_count * col_count)
    first_slot = replica * per_replica
    chosen = lax.dynamic_slice_in_dim(sources, first_slot * owner_count, per_replica * owner_count)
    usable = lax.dynamic_slice_in_dim(filled, first_slot * owner_count, per_replica * owner_count)
    picked = jnp.take(flattened, chosen, axis=0)
    picked = jnp.where(usable[:, None], picked, jnp.zeros_like(picked))
    outgoing = picked.reshape(per_replica, owner_count, row_count, col_count)
    received = lax.all_to_all(outgoing, "fsdp", split_axis=1, concat_axis=1, tiled=True)
    items = received.shape[0]
    matrices = received.reshape(items, owner_count * row_count, col_count)
    result = jax.vmap(newton)(matrices)
    finished = result.reshape(items, owner_count, row_count, col_count)
    owned_update = finished.reshape(per_replica, owner_count * row_count, col_count)
    returned = lax.all_to_all(finished, "fsdp", split_axis=1, concat_axis=1, tiled=True)
    complete = lax.all_gather(returned, "rep", axis=0, tiled=True)
    stacked = complete.reshape(capacity * owner_count, row_count, col_count)
    update = jnp.take(stacked, position, axis=0)
    return (new_momentum, update, owned_update)


def solution(mesh):
    in_specs = (P(None, "fsdp", None), P(None, "fsdp", None), P())
    out_specs = (P(None, "fsdp", None), P(None, "fsdp", None), P(("fsdp", "rep"), None, None))
    return jax.shard_map(local, mesh=mesh, in_specs=in_specs, out_specs=out_specs, check_vma=False)
```

profile of v0, /device:TPU:1, one launch (start us, length us, event | category | flops | bytes accessed | tf_op | source)
XLA Modules:
  0.0 174.7 jit_solution(12986220659537661177)
XLA Ops:
  7.2 0.9 convert_reduce_fusion
  8.1 0.7 compare_and_fusion.1
  9.0 5.5 %fusion = (bf16[128,4,2048]{2,1,0:T(4,128)(2,1)S(1)}, f32[128,4,2048]{2,1,0:T(4,128)}) fusion(bf16[128,4,2048]{2,1,0:T(4,128)(2,1)} %param.3, f32[128,4,2048]{2,1,0:T(4,128)} %param.4), kind=kLoop, calls=%fused_computation.4 | loop fusion | flops 6291456 | bytes 12582912 | tf_op jit(solution)/shard_map/convert_element_type | solution.py:36
  14.6 1.4 copy.14
  16.1 1.2 gather_fusion
  17.3 0.8 gather.11
  18.2 0.7 fusion.18
  18.9 41.3 %all_to_all.10 = bf16[1,64,4,2048]{3,2,0,1:T(4,128)(2,1)S(1)} all-to-all(bf16[1,64,4,2048]{3,2,0,1:T(4,128)(2,1)S(1)} %fusion.18), channel_id=1, replica_groups=mesh['fsdp'=64,'rep'=4] {'fsdp'}, dimensions={1} | all-to-all | bytes 2097152 | tf_op jit(solution)/shard_map/all_to_all | solution.py:53
  60.2 1.7 fusion.6
  62.6 0.6 fusion.7
  64.0 0.6 fusion.1
  64.6 0.5 convolution_convert_fusion.3
  65.0 0.6 fusion.2
  66.1 0.6 fusion.3
  66.7 0.5 convolution_convert_fusion.1
  67.2 0.6 fusion.4
  67.7 0.5 convolution_convert_fusion
  68.2 0.6 fusion.5
  69.3 34.7 %all_to_all.11 = bf16[1,64,4,2048]{3,2,0,1:T(4,128)(2,1)S(1)} all-to-all(bf16[1,64,4,2048]{3,2,0,1:T(4,128)(2,1)S(1)} %bitcast.39), channel_id=1, replica_groups=mesh['fsdp'=64,'rep'=4] {'fsdp'}, dimensions={1} | all-to-all | bytes 2097152 | tf_op jit(solution)/shard_map/all_to_all | solution.py:59
  104.0 1.5 copy.12
  105.6 48.0 %all-gather.2.cloned.1.call-done = bf16[4,64,4,2048]{3,1,2,0:T(8,128)(2,1)} async-done(((bf16[1,64,4,2048]{3,1,2,0:T(8,128)(2,1)}), bf16[4,64,4,2048]{3,1,2,0:T(8,128)(2,1)}) %all-gather.2.cloned.1.call-update) | async-done | bytes 4194320 | tf_op jit(solution)/shard_map/all_gather | solution.py:60
  153.6 7.4 %copy.13 = bf16[4,64,4,2048]{3,2,1,0:T(4,128)(2,1)} copy(bf16[4,64,4,2048]{3,1,2,0:T(8,128)(2,1)} %all-gather.2.cloned.1.call-done) | data formatting | bytes 8388608 | tf_op jit(solution)/shard_map/all_gather | solution.py:60
  161.0 4.5 %gather_fusion.1 = bf16[128,4,2048]{2,1,0:T(4,128)(2,1)S(1)} fusion(bf16[256,4,2048]{2,1,0:T(4,128)(2,1)} %bitcast.37, s32[1024]{0:T(1024)S(1)} %pad_clamp_fusion), kind=kCustom, calls=%fused_computation.1 | custom fusion | bytes 4194816 | tf_op jit(solution)/shard_map/jit(_take)/gather | solution.py:62
  165.5 2.4 %broadcast_select_fusion = bf16[128,4,2048]{2,1,0:T(4,128)(2,1)} fusion(bf16[128,4,2048]{2,1,0:T(4,128)(2,1)S(1)} %gather_fusion.1, pred[128]{0:T(512)(128)(4,1)S(1)} %get-tuple-element.3), kind=kLoop, calls=%fused_computation.19 | loop fusion | flops 1048576 | bytes 4194432 | tf_op jit(solution)/shard_map/jit(_take)/select_n | solution.py:62
  (15 shorter events, 2.1 us)
Async XLA Ops:
  7.2 146.4 %all-gather.2.cloned.1.call-start = ((), (), s32[]{:S(2)}) async-start(), calls=%async_computation.2 | async-start | bytes 5242880 | tf_op jit(solution)/shard_map/all_gather | solution.py:60
  68.8 35.2 %copy-start = (bf16[256,2048]{1,0:T(8,128)(2,1)}, bf16[256,2048]{1,0:T(8,128)(2,1)S(1)}, u32[]{:S(2)}) copy-start(bf16[256,2048]{1,0:T(8,128)(2,1)S(1)} %fusion.5) | copy-start | bytes 3145732
Sparse Core Ops, SparseCore 0:
  105.7 47.8 all-gather.1
where the time goes:
time: 175 us
  blocking collectives  76.1 us (43%)
  waiting for transfers between devices  48 us (27%)
  local copies, waits for them, and re-layouts  17.7 us (10%)
  between operations  14.9 us (9%)
  other arithmetic  12.8 us (7%)
  matrix products  5.23 us (3%)
    all_gather x1, waiting for transfers between devices, local(): complete = lax.all_gather(returned, 'rep', axis=0, tiled=True)  48 us
    all_to_all x1, blocking collectives, local(): lax.all_to_all(outgoing, 'fsdp', split_axis=1, concat_axis=1, tiled=True)  41.3 us
    all_to_all x1, blocking collectives, local(): lax.all_to_all(finished, 'fsdp', split_axis=1, concat_axis=1, tiled=True)  34.7 us
    all_gather x1, local copies, waits for them, and re-layouts, local(): complete = lax.all_gather(returned, 'rep', axis=0, tiled=True)  7.43 us
    convert_element_type x1, other arithmetic, local(): (grad.astype(jnp.float32) + decay_rate * new_momentum).astype(jnp.bfloat16)  5.54 us
    gather x1, local copies, waits for them, and re-layouts, local(): update = jnp.take(stacked, position, axis=0)  4.52 us
  transfers between devices with their start and end apart: 1, of which 1 were waited for; matrix products, arithmetic and copies ran while one was open for 0% of the time, Pallas kernels for 0%

commit v1 on v0

--- a/solution.py
+++ b/solution.py
@@ -10,6 +10,36 @@
 quintic_a = 3.4445
 quintic_b = -4.775
 quintic_c = 2.0315
+
+
+def wait_paths_over_axis(array_in, d_out):
+    array_in = jnp.moveaxis(array_in, 0, d_out)
+    vec_out = array_in.shape
+    local_next = array_in.reshape(
+        *vec_out[:d_out], vec_out[d_out] * vec_out[d_out + 1], *vec_out[d_out + 2 :]
+    )
+    return local_next
+
+
+def reach_squares_over_axis(block_in, dev_axis, on_dim=0):
+    shares = lax.axis_size(dev_axis)
+    heap = [(dev, (dev + 1) % shares) for dev in range(shares)]
+    found = [(u, ix) for ix, u in heap]
+    y, back = ([], [])
+    for kk in range(shares - 1):
+        if kk % 2 == 0:
+            z = lax.ppermute(y[-1] if y else block_in, axis_name=dev_axis, perm=heap)
+            y.append(z)
+        else:
+            a_now = lax.ppermute(back[-1] if back else block_in, axis_name=dev_axis, perm=found)
+            back.append(a_now)
+    arr_next = jnp.stack([*y[::-1], block_in, *back], 0)
+    val2 = len(y)
+    r1 = lax.axis_index(dev_axis)
+    local_part = r1 - val2
+    arr_next = arr_next[(jnp.arange(shares) - local_part) % shares]
+    e_next = wait_paths_over_axis(arr_next, on_dim)
+    return e_next
 
 
 def newton(blended):
@@ -57,7 +87,7 @@
     finished = result.reshape(items, owner_count, row_count, col_count)
     owned_update = finished.reshape(per_replica, owner_count * row_count, col_count)
     returned = lax.all_to_all(finished, "fsdp", split_axis=1, concat_axis=1, tiled=True)
-    complete = lax.all_gather(returned, "rep", axis=0, tiled=True)
+    complete = reach_squares_over_axis(returned, "rep")
     stacked = complete.reshape(capacity * owner_count, row_count, col_count)
     update = jnp.take(stacked, position, axis=0)
     return (new_momentum, update, owned_update)

time: 175 us -> 169 us (0.966)
  between operations: 14.9 us -> 1.52 us
  other arithmetic: 12.8 us -> 18.8 us
  starting transfers between devices: 0.04 us -> 2.73 us
    ppermute x0 -> x3, waiting for transfers between devices: none -> 48.4 us  [the longest x2 48.4 us: reach_squares_over_axis(): z = lax.ppermute(y[-1] if y else block_in, axis_name=dev_axis, perm=heap)]
    all_gather x1 -> x0, waiting for transfers between devices: 48 us -> none  [local(): complete = lax.all_gather(returned, 'rep', axis=0, tiled=True)]
    gather x0 -> x1, local copies, waits for them, and re-layouts: none -> 7.52 us  [reach_squares_over_axis(): arr_next = arr_next[(jnp.arange(shares) - local_part) % shares]]
    all_gather x1 -> x0, local copies, waits for them, and re-layouts: 7.43 us -> none  [local(): complete = lax.all_gather(returned, 'rep', axis=0, tiled=True)]
    another operation x0 -> x1, other arithmetic: none -> 5.98 us  [reach_squares_over_axis(): arr_next = jnp.stack([*y[::-1], block_in, *back], 0)]
    ppermute x0 -> x3, starting transfers between devices: none -> 2.73 us  [the longest x1 1.43 us: reach_squares_over_axis(): lax.ppermute(back[-1] if back else block_in, axis_name=dev_axis, perm=found)]
  transfers between devices with their start and end apart: 1 -> 3, of which waited for: 1 -> 2; matrix products, arithmetic and copies ran while one was open for 0% -> 0% of each run, Pallas kernels for 0% -> 0%
where the time goes in v1:
time: 169 us
  blocking collectives  76.1 us (45%)
  waiting for transfers between devices  48.4 us (29%)
  other arithmetic  18.8 us (11%)
  local copies, waits for them, and re-layouts  16.3 us (10%)
  matrix products  5.23 us (3%)
  starting transfers between devices  2.73 us (2%)
    ppermute x2, waiting for transfers between devices, reach_squares_over_axis(): z = lax.ppermute(y[-1] if y else block_in, axis_name=dev_axis, perm=heap)  48.4 us
    all_to_all x1, blocking collectives, local(): lax.all_to_all(outgoing, 'fsdp', split_axis=1, concat_axis=1, tiled=True)  41.3 us
    all_to_all x1, blocking collectives, local(): lax.all_to_all(finished, 'fsdp', split_axis=1, concat_axis=1, tiled=True)  34.7 us
    gather x1, local copies, waits for them, and re-layouts, reach_squares_over_axis(): arr_next = arr_next[(jnp.arange(shares) - local_part) % shares]  7.52 us
    another operation x1, other arithmetic, reach_squares_over_axis(): arr_next = jnp.stack([*y[::-1], block_in, *back], 0)  5.98 us
    convert_element_type x1, other arithmetic, local(): (grad.astype(jnp.float32) + decay_rate * new_momentum).astype(jnp.bfloat16)  5.54 us
    gather x1, local copies, waits for them, and re-layouts, local(): update = jnp.take(stacked, position, axis=0)  4.52 us
  transfers between devices with their start and end apart: 3, of which 2 were waited for; matrix products, arithmetic and copies ran while one was open for 0% of the time, Pallas kernels for 0%

profile of v1, /device:TPU:1, one launch (start us, length us, event | category | flops | bytes accessed | tf_op | source)
XLA Modules:
  0.0 169.0 jit_solution(10908245870579613609)
XLA Ops:
  0.6 0.9 convert_reduce_fusion
  1.5 0.7 compare_and_fusion.1
  2.4 5.5 %fusion = (bf16[128,4,2048]{2,1,0:T(4,128)(2,1)S(1)}, f32[128,4,2048]{2,1,0:T(4,128)}) fusion(bf16[128,4,2048]{2,1,0:T(4,128)(2,1)} %param.3, f32[128,4,2048]{2,1,0:T(4,128)} %param.4), kind=kLoop, calls=%fused_computation.5 | loop fusion | flops 6291456 | bytes 12582912 | tf_op jit(solution)/shard_map/convert_element_type | solution.py:66
  8.0 1.4 copy.12
  9.5 1.2 gather_fusion
  10.7 0.8 gather.14
  11.6 0.7 fusion.18
  12.3 41.3 %all_to_all.10 = bf16[1,64,4,2048]{3,2,0,1:T(4,128)(2,1)S(1)} all-to-all(bf16[1,64,4,2048]{3,2,0,1:T(4,128)(2,1)S(1)} %fusion.18), channel_id=1, replica_groups=mesh['fsdp'=64,'rep'=4] {'fsdp'}, dimensions={1} | all-to-all | bytes 2097152 | tf_op jit(solution)/shard_map/all_to_all | solution.py:83
  53.7 1.7 fusion.6
  56.0 0.6 fusion.7
  57.4 0.6 fusion.1
  58.5 0.6 fusion.2
  59.5 0.6 fusion.3
  60.6 0.6 fusion.4
  61.6 0.6 fusion.5
  62.7 34.7 %all_to_all.11 = bf16[1,64,4,2048]{3,2,0,1:T(4,128)(2,1)S(1)} all-to-all(bf16[1,64,4,2048]{3,2,0,1:T(4,128)(2,1)S(1)} %bitcast.48), channel_id=1, replica_groups=mesh['fsdp'=64,'rep'=4] {'fsdp'}, dimensions={1} | all-to-all | bytes 2097152 | tf_op jit(solution)/shard_map/all_to_all | solution.py:89
  97.4 1.3 collective-permute-start
  98.7 1.4 collective-permute-start.2
  100.1 23.3 %collective-permute-done = bf16[1,64,4,2048]{3,2,1,0:T(4,128)(2,1)S(1)} collective-permute-done((bf16[1,64,4,2048]{3,2,1,0:T(4,128)(2,1)S(1)}, bf16[1,64,4,2048]{3,2,1,0:T(4,128)(2,1)S(1)}, u32[]{:S(2)}, u32[]{:S(2)}) %collective-permute-start) | collective-permute-done | bytes 1048608 | tf_op jit(solution)/shard_map/ppermute | solution.py:31
  123.5 25.1 %collective-permute-done.1 = bf16[1,64,4,2048]{3,2,1,0:T(4,128)(2,1)} collective-permute-done((bf16[1,64,4,2048]{3,2,1,0:T(4,128)(2,1)S(1)}, bf16[1,64,4,2048]{3,2,1,0:T(4,128)(2,1)}, u32[]{:S(2)}, u32[]{:S(2)}) %collective-permute-start.1) | collective-permute-done | bytes 1048608 | tf_op jit(solution)/shard_map/ppermute | solution.py:31
  148.6 6.0 %maximum_bitcast_fusion = bf16[4,64,4,2048]{3,2,1,0:T(4,128)(2,1)} fusion(bf16[1,1,64,4,2048]{4,3,2,1,0:T(4,128)(2,1)S(1)} %bitcast.53, bf16[1,1,64,4,2048]{4,3,2,1,0:T(4,128)(2,1)S(1)} %bitcast.50, bf16[1,1,64,4,2048]{4,3,2,1,0:T(4,128)(2,1)S(1)} %bitcast.52, bf16[1,1,64,4,2048]{4,3,2,1,0:T(4,128)(2,1)} %bitcast.3), kind=kLoop, calls=%fused_computation.6 | loop fusion | flops 6291456 | bytes 8388608 | tf_op jit(solution)/shard_map/stack | solution.py:36
  154.6 7.5 %gather_fusion.1 = bf16[4,64,4,2048]{3,2,1,0:T(4,128)(2,1)} fusion(bf16[4,64,4,2048]{3,2,1,0:T(4,128)(2,1)} %maximum_bitcast_fusion, s32[1024]{0:T(1024)S(1)} %pad_clamp_fusion.1), kind=kCustom, calls=%fused_computation.1 | custom fusion | bytes 8388624 | tf_op jit(solution)/shard_map/gather | solution.py:40
  162.1 4.5 %gather_fusion.2 = bf16[128,4,2048]{2,1,0:T(4,128)(2,1)S(1)} fusion(bf16[256,4,2048]{2,1,0:T(4,128)(2,1)} %bitcast.46, s32[1024]{0:T(1024)S(1)} %pad_clamp_fusion), kind=kCustom, calls=%fused_computation.2 | custom fusion | bytes 4194816 | tf_op jit(solution)/shard_map/jit(_take)/gather | solution.py:92
  166.6 2.4 %broadcast_select_fusion = bf16[128,4,2048]{2,1,0:T(4,128)(2,1)} fusion(bf16[128,4,2048]{2,1,0:T(4,128)(2,1)S(1)} %gather_fusion.2, pred[128]{0:T(512)(128)(4,1)S(1)} %get-tuple-element.3), kind=kLoop, calls=%fused_computation.21 | loop fusion | flops 1048576 | bytes 4194432 | tf_op jit(solution)/shard_map/jit(_take)/select_n | solution.py:92
  (20 shorter events, 3.5 us)
Async XLA Ops:
  62.2 35.2 %copy-start = (bf16[256,2048]{1,0:T(8,128)(2,1)}, bf16[256,2048]{1,0:T(8,128)(2,1)S(1)}, u32[]{:S(2)}) copy-start(bf16[256,2048]{1,0:T(8,128)(2,1)S(1)} %fusion.5) | copy-start | bytes 3145732
  97.4 26.0 %collective-permute-start = (bf16[1,64,4,2048]{3,2,1,0:T(4,128)(2,1)S(1)}, bf16[1,64,4,2048]{3,2,1,0:T(4,128)(2,1)S(1)}, u32[]{:S(2)}, u32[]{:S(2)}) collective-permute-start(bf16[1,64,4,2048]{3,2,1,0:T(4,128)(2,1)S(1)} %bitcast.49), channel_id=1, source_target_pairs={{0,1},{1,2},{2,3},{3,0},{4,5},{5,6},{6,7},{7,4},{8,9},{9,10},{10,1... | collective-permute-start | bytes 3145736 | tf_op jit(solution)/shard_map/ppermute | solution.py:31
  98.7 24.8 %collective-permute-start.2 = (bf16[1,64,4,2048]{3,2,0,1:T(4,128)(2,1)S(1)}, bf16[1,64,4,2048]{3,2,0,1:T(4,128)(2,1)S(1)}, u32[]{:S(2)}, u32[]{:S(2)}) collective-permute-start(bf16[1,64,4,2048]{3,2,0,1:T(4,128)(2,1)S(1)} %all_to_all.11), channel_id=1, source_target_pairs={{1,0},{2,1},{3,2},{0,3},{5,4},{6,5},{7,6},{4,7},{9,8},{10,9},{11,1... | collective-permute-start | bytes 3145736 | tf_op jit(solution)/shard_map/ppermute | solution.py:34
  123.4 25.2 %collective-permute-start.1 = (bf16[1,64,4,2048]{3,2,1,0:T(4,128)(2,1)S(1)}, bf16[1,64,4,2048]{3,2,1,0:T(4,128)(2,1)}, u32[]{:S(2)}, u32[]{:S(2)}) collective-permute-start(bf16[1,64,4,2048]{3,2,1,0:T(4,128)(2,1)S(1)} %collective-permute-done), channel_id=1, source_target_pairs={{0,1},{1,2},{2,3},{3,0},{4,5},{5,6},{6,7},{7,4},{8,9},{9,10},{10,1... | collective-permute-start | bytes 3145736 | tf_op jit(solution)/shard_map/ppermute | solution.py:31
